TPU v7x, 32 devices: a whole 2x2x4 slice. The times are simulated.
32 devices in a mesh: tm: 4 (over y, core), space: 8 (over z, x).
Axes of the slice: x: 2, y: 2, z: 4, core: 2. Of those that a mesh axis runs over, the one named last changes fastest.
Arguments:
- initial: float32 [4, 128, 8192], P('tm', None, 'space'), may hold values from -324 to 324
- rhs: float32 [4, 128, 8192], P('tm', None, 'space'), may hold values from -324 to 324
- coef: float32 [8192], P('space'), may hold values from 0.5 to 4
- stiffness: float32 [128, 128], replicated, may hold values from -0.5 to 0.5
- block_inverse: float32 [128, 128], replicated, may hold values from -0.5 to 0.5
- face_proj: float32 [192, 128], replicated, may hold values from -0.5 to 0.5
- lift: float32 [128, 192], replicated, may hold values from -0.4375 to 0.4375
- time_lift: float32 [128, 64], replicated, may hold values from -0.75 to 0.75
- neighbour: int32 [6, 8192], P(None, 'space'), may hold values from 0 to 6399, as said below
- boundary: int32 [6, 8192], P(None, 'space'), may hold values from 0 to 1, as said below
- send_list: int32 [2048], P('space'), may hold values from 0 to 2047, as said below
Outputs:
- smoothed: float32 [4, 128, 8192], P('tm', None, 'space')
- indicator: float32 [4, 8192], P('tm', 'space')
- estimate: float32 [1], replicated
Inputs may be any that keep to these rules, and one draw needn't show every extreme that they name: `neighbour`: the elements form a structured hexahedral grid numbered in a random order inside each partition; partition p holds 8 element layers and meets partitions p - 1 and p + 1 across 128 faces each, listed in the same order on both sides. Interior faces point to the opposite face of the neighbouring element; faces toward another partition point to columns 6144 and above; boundary faces may point anywhere. `boundary`: marks the outer faces of the whole grid. `send_list`: the first 128 entries of a partition list its faces facing the lower partition, the next 128 those facing the upper one, as columns of its own pool below 2048.
All inputs are finite; a program needn't handle non-finite values.
Results may differ from a plain program's by a relative error of at most 0.000059.
Values sent between devices are 32-bit elements; how exact they have to be, the bound alone decides.
No kernel may reach another device: no remote copies, remote signals or barrier semaphores. Data moves between devices by JAX's collectives and lax.ppermute only.
A program may use at most 64 MiB of HBM per device.

v0:
```python
import jax
import jax.numpy as jnp
from jax import lax
from jax.sharding import PartitionSpec as P


def padded(x, sides, width):
    for axis, dim in sides:
        devices, length = (lax.axis_size(axis), x.shape[dim])
        up = [(i, (i + 1) % devices) for i in range(devices - 1)]
        down = [(j, i) for i, j in up]
        last = lax.slice_in_dim(x, length - width, length, axis=dim)
        initial = lax.slice_in_dim(x, 0, width, axis=dim)
        before = lax.ppermute(last, axis, up)
        after = lax.ppermute(initial, axis, down)
        x = jnp.concatenate([before, x, after], axis=dim)
    return x


def shifted(value, axis, steps):
    count = lax.axis_size(axis)
    initial, last = (max(0, -steps), min(count, count - steps))
    return lax.ppermute(value, axis, [(source, source + steps) for source in range(initial, last)])


def on_device(
    initial,
    rhs,
    coef,
    stiffness,
    block_inverse,
    face_proj,
    lift,
    time_lift,
    neighbour,
    boundary,
    send_list,
):
    start_field = initial[0]
    source = rhs[0]
    elements = start_field.shape[1]
    half_dofs = start_field.shape[0] // 2
    face_dofs = face_proj.shape[0] // 6
    border = send_list.shape[0] // 2
    column_ids = neighbour.reshape(6 * elements)
    open_faces = jnp.tile(1.0 - boundary.astype(jnp.float32), (face_dofs, 1))

    def operate(vector):
        traces = jnp.dot(face_proj, vector, precision=lax.Precision.HIGHEST)
        trace_pool = traces.reshape(face_dofs, 6 * elements)
        outbound = jnp.take(trace_pool, send_list, axis=1)
        received = padded(outbound, (("space", 1),), border)
        from_lower = received[:, :border]
        from_upper = received[:, 3 * border :]
        prev_end = shifted(vector[half_dofs:], "tm", 1)
        ext_pool = jnp.concatenate([trace_pool, from_lower, from_upper], axis=1)
        outside = jnp.take(ext_pool, column_ids, axis=1).reshape(face_dofs * 6, elements)
        face_jump = traces - outside * open_faces
        time_jump = vector[:half_dofs] - prev_end
        applied = coef * jnp.dot(stiffness, vector, precision=lax.Precision.HIGHEST)
        applied = applied + jnp.dot(lift, face_jump, precision=lax.Precision.HIGHEST)
        applied = applied + jnp.dot(time_lift, time_jump, precision=lax.Precision.HIGHEST)
        return (applied, face_jump, time_jump)

    applied_base, base_jump, base_time = operate(start_field)
    residual = source - applied_base
    direction = jnp.dot(block_inverse, residual, precision=lax.Precision.HIGHEST) / coef
    image, step_jump, step_time = operate(direction)
    cross_sum = jnp.sum(residual * image)
    image_sum = jnp.sum(image * image)
    total_cross, total_image = lax.psum((cross_sum, image_sum), ("tm", "space"))
    step_size = total_cross / total_image
    smoothed = start_field + step_size * direction
    new_residual = residual - step_size * image
    new_jump = base_jump + step_size * step_jump
    new_time = base_time + step_size * step_time
    element_eta = (
        jnp.sum(new_residual * new_residual, axis=0)
        + 0.5 * jnp.sum(new_jump * new_jump, axis=0)
        + jnp.sum(new_time * new_time, axis=0)
    )
    eta_total = lax.psum(jnp.sum(element_eta), ("tm", "space"))
    element_count = elements * lax.axis_size("tm") * lax.axis_size("space")
    indicator = element_eta * element_count / eta_total
    estimate = jnp.sqrt(eta_total / element_count).reshape(1)
    return (smoothed[None], indicator[None], estimate)


def solution(mesh):
    placed = (
        P("tm", None, "space"),
        P("tm", None, "space"),
        P("space"),
        P(),
        P(),
        P(),
        P(),
        P(),
        P(None, "space"),
        P(None, "space"),
        P("space"),
    )
    return jax.shard_map(
        on_device,
        mesh=mesh,
        in_specs=placed,
        out_specs=(P("tm", None, "space"), P("tm", "space"), P()),
        check_vma=False,
    )
```

profile of v0, /device:TPU:0, one launch (start us, length us, event | category | flops | bytes accessed | tf_op | source)
XLA Modules:
  0.0 214.1 jit_solution(13432390113323997010)
XLA Ops:
  2.1 1.8 fusion.4
  4.8 1.3 reshape.74
  6.0 2.0 copy.37
  9.7 4.9 %collective-permute-start = (f32[32,128]{0,1:T(8,128)}, f32[32,128]{0,1:T(8,128)S(1)}, u32[]{:S(2)}, u32[]{:S(2)}) collective-permute-start(f32[32,128]{0,1:T(8,128)} %get-tuple-element.11), channel_id=1, source_target_pairs={{0,1},{1,2},{2,3},{3,4},{4,5},{5,6},{6,7},{8,9},{9,10},{10,11},{11... | collective-permute-start | bytes 49160 | tf_op jit(solution)/shard_map/ppermute | solution.py:14
  14.5 1.3 collective-permute-start.1
  15.8 1.7 slice_bitcast_fusion
  17.5 2.2 %collective-permute-start.2 = (f32[64,1024]{1,0:T(8,128)}, f32[64,1024]{1,0:T(8,128)}, u32[]{:S(2)}, u32[]{:S(2)}) collective-permute-start(f32[64,1024]{1,0:T(8,128)} %slice_bitcast_fusion), channel_id=1, source_target_pairs={{0,8},{8,16},{16,24},{1,9},{9,17},{17,25},{2,10},{10,18},{18,26},{... | collective-permute-start | bytes 786440 | tf_op jit(solution)/shard_map/ppermute | solution.py:23
  20.5 2.4 %convolution_multiply_fusion.1 = f32[128,1024]{1,0:T(8,128)} fusion(f32[128,128]{1,0:T(8,128)S(1)} %copy-done.22, f32[1,128,1024]{2,1,0:T(8,128)} %param.15, f32[1024]{0:T(1024)S(1)} %copy-done.27), kind=kOutput, calls=%fused_computation.18 | convolution fusion | flops 201457664 | bytes 1118208 | tf_op jit(solution)/shard_map/dot_general | solution.py:60
  24.0 2.2 %tile.10 = f32[192,1024]{1,0:T(8,128)} reshape(f32[32,6,1024]{2,1,0:T(8,128)} %tile.4) | data formatting | bytes 1572864 | tf_op jit(solution)/shard_map/tile | solution.py:46
  26.3 2.1 pad_maximum_fusion
  28.4 20.9 %gather_fusion.1 = f32[6144,32]{1,0:T(8,128)} fusion(f32[32,6400]{0,1:T(8,128)S(1)} %pad_maximum_fusion, s32[6144]{0:T(1024)S(1)} %fusion.8), kind=kCustom, calls=%fused_computation.1.clone | custom fusion | bytes 1597440 | tf_op jit(solution)/shard_map/jit(_take)/gather | solution.py:57
  49.3 5.8 %select_bitcast_fusion.1 = f32[32,6144]{0,1:T(8,128)} fusion(f32[6144,32]{1,0:T(8,128)} %gather_fusion.1, pred[6144]{0:T(1024)(128)(4,1)S(1)} %compare_and_fusion), kind=kLoop, calls=%fused_computation.7 | loop fusion | flops 196608 | bytes 1579008 | tf_op jit(solution)/shard_map/jit(_take)/select_n | solution.py:57
  55.1 3.2 %copy.38 = f32[32,6144]{1,0:T(8,128)} copy(f32[32,6144]{0,1:T(8,128)} %select_bitcast_fusion.1) | data formatting | bytes 1572864 | tf_op jit(solution)/shard_map/jit(_take)/select_n | solution.py:57
  58.4 1.4 reshape.76
  59.8 1.9 fusion.2
  61.7 1.6 fusion.3
  67.3 1.3 reshape.77
  68.5 2.0 copy.40
  71.4 4.4 %collective-permute-start.3 = (f32[32,128]{0,1:T(8,128)S(1)}, f32[32,128]{0,1:T(8,128)S(1)}, u32[]{:S(2)}, u32[]{:S(2)}) collective-permute-start(f32[32,128]{0,1:T(8,128)S(1)} %get-tuple-element.9), channel_id=1, source_target_pairs={{0,1},{1,2},{2,3},{3,4},{4,5},{5,6},{6,7},{8,9},{9,10},{10,11},{11... | collective-permute-start | bytes 49160 | tf_op jit(solution)/shard_map/ppermute | solution.py:14
  75.8 1.3 collective-permute-start.4
  77.1 2.4 %convolution_multiply_fusion = f32[1024,128]{0,1:T(8,128)} fusion(f32[1024,128]{0,1:T(8,128)} %copy-done.12, f32[128,128]{1,0:T(8,128)S(1)} %copy-done.23, f32[1024]{0:T(1024)S(1)} %copy-done.27), kind=kOutput, calls=%fused_computation.14 | convolution fusion | flops 201457664 | bytes 1118208 | tf_op jit(solution)/shard_map/dot_general | solution.py:60
  79.5 1.7 slice.53
  81.2 3.9 %collective-permute-start.5 = (f32[64,1024]{1,0:T(8,128)}, f32[64,1024]{1,0:T(8,128)}, u32[]{:S(2)}, u32[]{:S(2)}) collective-permute-start(f32[64,1024]{1,0:T(8,128)} %slice.53), channel_id=1, source_target_pairs={{0,8},{8,16},{16,24},{1,9},{9,17},{17,25},{2,10},{10,18},{18,26},{... | collective-permute-start | bytes 786440 | tf_op jit(solution)/shard_map/ppermute | solution.py:23
  85.1 2.1 pad_maximum_fusion.1
  87.2 20.9 %gather_fusion.3 = f32[6144,32]{1,0:T(8,128)} fusion(f32[32,6400]{0,1:T(8,128)S(1)} %pad_maximum_fusion.1, s32[6144]{0:T(1024)S(1)} %fusion.8), kind=kCustom, calls=%fused_computation.3.clone | custom fusion | bytes 1597440 | tf_op jit(solution)/shard_map/jit(_take)/gather | solution.py:57
  108.1 5.8 %select_bitcast_fusion = f32[32,6144]{0,1:T(8,128)} fusion(f32[6144,32]{1,0:T(8,128)} %gather_fusion.3, pred[6144]{0:T(1024)(128)(4,1)S(1)} %compare_and_fusion), kind=kLoop, calls=%fused_computation.6 | loop fusion | flops 196608 | bytes 1579008 | tf_op jit(solution)/shard_map/jit(_take)/select_n | solution.py:57
  113.9 2.5 %copy.41 = f32[32,6144]{1,0:T(8,128)S(1)} copy(f32[32,6144]{0,1:T(8,128)} %select_bitcast_fusion) | data formatting | bytes 1572864 | tf_op jit(solution)/shard_map/jit(_take)/select_n | solution.py:57
  117.5 2.0 convolution_add_fusion.1
  119.5 3.1 %multiply_reduce_fusion.2 = (f32[]{:T(128)}, f32[]{:T(128)}, f32[128,1024]{1,0:T(8,128)}) fusion(f32[128,1024]{1,0:T(8,128)S(1)} %copy-done.16, f32[1024,128]{0,1:T(8,128)S(1)} %convolution_add_fusion.1, f32[128,64]{0,1:T(8,128)S(1)} %copy-done.25, f32[64,1024]{1,0:T(8,128)} %collective-permute-done.5, f32[128,1024]{1,0:T(8,128)S(1)} %bitcast.58), kind=kOutput, calls=%fused_computation.29 | convolution fusion | flops 101384192 | bytes 2129928 | tf_op jit(solution)/shard_map/dot_general | solution.py:62
  122.6 42.4 %all-reduce = (f32[]{:T(128)}, f32[]{:T(128)}) all-reduce(f32[]{:T(128)} %get-tuple-element.6, f32[]{:T(128)} %get-tuple-element.5), channel_id=1, replica_groups=mesh['tm'=4,'space'=8] {'tm','space'}, use_global_device_ids=true, to_apply=%region_1.4 | all-reduce | flops 2 | bytes 16 | tf_op jit(solution)/shard_map/psum | solution.py:71
  166.4 1.9 multiply_reduce_fusion
  171.0 40.0 %psum.23 = f32[]{:T(128)} all-reduce(f32[]{:T(128)} %fusion.9), channel_id=1, replica_groups=mesh['tm'=4,'space'=8] {'tm','space'}, use_global_device_ids=true, to_apply=%region_8.11 | all-reduce | flops 1 | bytes 8 | tf_op jit(solution)/shard_map/psum | solution.py:82
  (86 shorter events, 15.7 us)
Async XLA Ops:
  0.6 1.4 copy-start
  4.8 14.9 %copy-start.26 = (s32[6,1024]{1,0:T(8,128)S(1)}, s32[6,1024]{1,0:T(8,128)}, u32[]{:S(2)}) copy-start(s32[6,1024]{1,0:T(8,128)} %param.23) | copy-start | bytes 73732
  4.8 15.7 %copy-start.22 = (f32[128,128]{1,0:T(8,128)S(1)}, f32[128,128]{1,0:T(8,128)}, u32[]{:S(2)}) copy-start(f32[128,128]{1,0:T(8,128)} %param.18) | copy-start | bytes 196612
  4.8 15.7 %copy-start.27 = (f32[1024]{0:T(1024)S(1)}, f32[1024]{0:T(1024)}, u32[]{:S(2)}) copy-start(f32[1024]{0:T(1024)} %param.17) | copy-start | bytes 12292
  8.0 18.3 %copy-start.1 = (f32[32,6144]{0,1:T(8,128)}, f32[32,6144]{0,1:T(8,128)S(1)}, u32[]{:S(2)}) copy-start(f32[32,6144]{0,1:T(8,128)S(1)} %copy.37) | copy-start | bytes 2359300
  9.7 16.6 %collective-permute-start = (f32[32,128]{0,1:T(8,128)}, f32[32,128]{0,1:T(8,128)S(1)}, u32[]{:S(2)}, u32[]{:S(2)}) collective-permute-start(f32[32,128]{0,1:T(8,128)} %get-tuple-element.11), channel_id=1, source_target_pairs={{0,1},{1,2},{2,3},{3,4},{4,5},{5,6},{6,7},{8,9},{9,10},{10,11},{11... | collective-permute-start | bytes 49160 | tf_op jit(solution)/shard_map/ppermute | solution.py:14
  14.5 11.7 %collective-permute-start.1 = (f32[32,128]{0,1:T(8,128)}, f32[32,128]{0,1:T(8,128)S(1)}, u32[]{:S(2)}, u32[]{:S(2)}) collective-permute-start(f32[32,128]{0,1:T(8,128)} %get-tuple-element.12), channel_id=1, source_target_pairs={{1,0},{2,1},{3,2},{4,3},{5,4},{6,5},{7,6},{9,8},{10,9},{11,10},{12... | collective-permute-start | bytes 49160 | tf_op jit(solution)/shard_map/ppermute | solution.py:15
  17.5 44.2 %collective-permute-start.2 = (f32[64,1024]{1,0:T(8,128)}, f32[64,1024]{1,0:T(8,128)}, u32[]{:S(2)}, u32[]{:S(2)}) collective-permute-start(f32[64,1024]{1,0:T(8,128)} %slice_bitcast_fusion), channel_id=1, source_target_pairs={{0,8},{8,16},{16,24},{1,9},{9,17},{17,25},{2,10},{10,18},{18,26},{... | collective-permute-start | bytes 786440 | tf_op jit(solution)/shard_map/ppermute | solution.py:23
  55.1 4.6 %copy-start.4 = (f32[192,1024]{1,0:T(8,128)S(1)}, f32[192,1024]{1,0:T(8,128)}, u32[]{:S(2)}) copy-start(f32[192,1024]{1,0:T(8,128)} %copy-done.3) | copy-start | bytes 2359300
  55.1 4.6 %copy-start.6 = (f32[192,1024]{1,0:T(8,128)S(1)}, f32[192,1024]{1,0:T(8,128)}, u32[]{:S(2)}) copy-start(f32[192,1024]{1,0:T(8,128)} %tile.10) | copy-start | bytes 2359300
  55.1 4.6 %copy-start.19 = (f32[128,1024]{1,0:T(8,128)S(1)}, f32[128,1024]{1,0:T(8,128)}, u32[]{:S(2)}) copy-start(f32[128,1024]{1,0:T(8,128)} %convolution_multiply_fusion.1) | copy-start | bytes 1572868
  58.4 3.3 %copy-start.10 = (f32[1,128,1024]{2,1,0:T(8,128)S(1)}, f32[1,128,1024]{2,1,0:T(8,128)}, u32[]{:S(2)}) copy-start(f32[1,128,1024]{2,1,0:T(8,128)} %param.15) | copy-start | bytes 1572868
  59.8 5.0 %copy-start.14 = (f32[192,1024]{1,0:T(8,128)}, f32[192,1024]{1,0:T(8,128)S(1)}, u32[]{:S(2)}) copy-start(f32[192,1024]{1,0:T(8,128)S(1)} %reshape.76) | copy-start | bytes 2359300
  59.8 1.9 copy-start.21
  59.8 1.9 copy-start.24
  59.8 4.3 %copy-start.28 = (f32[128,128]{1,0:T(8,128)S(1)}, f32[128,128]{1,0:T(8,128)}, u32[]{:S(2)}) copy-start(f32[128,128]{1,0:T(8,128)} %param.19) | copy-start | bytes 196612
  66.4 0.9 copy-start.8
  67.3 9.8 %copy-start.23 = (f32[128,128]{1,0:T(8,128)S(1)}, f32[128,128]{1,0:T(8,128)}, u32[]{:S(2)}) copy-start(f32[128,128]{1,0:T(8,128)} %param.18) | copy-start | bytes 196612
  70.5 14.5 %copy-start.2 = (f32[32,6144]{0,1:T(8,128)}, f32[32,6144]{0,1:T(8,128)S(1)}, u32[]{:S(2)}) copy-start(f32[32,6144]{0,1:T(8,128)S(1)} %copy.40) | copy-start | bytes 2359300
  71.4 13.7 %collective-permute-start.3 = (f32[32,128]{0,1:T(8,128)S(1)}, f32[32,128]{0,1:T(8,128)S(1)}, u32[]{:S(2)}, u32[]{:S(2)}) collective-permute-start(f32[32,128]{0,1:T(8,128)S(1)} %get-tuple-element.9), channel_id=1, source_target_pairs={{0,1},{1,2},{2,3},{3,4},{4,5},{5,6},{6,7},{8,9},{9,10},{10,11},{11... | collective-permute-start | bytes 49160 | tf_op jit(solution)/shard_map/ppermute | solution.py:14
  75.8 9.3 %collective-permute-start.4 = (f32[32,128]{0,1:T(8,128)S(1)}, f32[32,128]{0,1:T(8,128)S(1)}, u32[]{:S(2)}, u32[]{:S(2)}) collective-permute-start(f32[32,128]{0,1:T(8,128)S(1)} %get-tuple-element.10), channel_id=1, source_target_pairs={{1,0},{2,1},{3,2},{4,3},{5,4},{6,5},{7,6},{9,8},{10,9},{11,10},{12... | collective-permute-start | bytes 49160 | tf_op jit(solution)/shard_map/ppermute | solution.py:15
  81.2 38.3 %collective-permute-start.5 = (f32[64,1024]{1,0:T(8,128)}, f32[64,1024]{1,0:T(8,128)}, u32[]{:S(2)}, u32[]{:S(2)}) collective-permute-start(f32[64,1024]{1,0:T(8,128)} %slice.53), channel_id=1, source_target_pairs={{0,8},{8,16},{16,24},{1,9},{9,17},{17,25},{2,10},{10,18},{18,26},{... | collective-permute-start | bytes 786440 | tf_op jit(solution)/shard_map/ppermute | solution.py:23
  113.9 3.6 %copy-start.7 = (f32[192,1024]{1,0:T(8,128)S(1)}, f32[192,1024]{1,0:T(8,128)}, u32[]{:S(2)}) copy-start(f32[192,1024]{1,0:T(8,128)} %tile.10) | copy-start | bytes 2359300
  113.9 3.6 %copy-start.9 = (f32[192,1024]{1,0:T(8,128)S(1)}, f32[192,1024]{1,0:T(8,128)}, u32[]{:S(2)}) copy-start(f32[192,1024]{1,0:T(8,128)} %copy-done.8) | copy-start | bytes 2359300
  113.9 3.6 %copy-start.18 = (f32[1024,128]{0,1:T(8,128)S(1)}, f32[1024,128]{0,1:T(8,128)}, u32[]{:S(2)}) copy-start(f32[1024,128]{0,1:T(8,128)} %convolution_multiply_fusion) | copy-start | bytes 1572868
  116.4 3.1 %copy-start.13 = (f32[1024,128]{0,1:T(8,128)S(1)}, f32[1024,128]{0,1:T(8,128)}, u32[]{:S(2)}) copy-start(f32[1024,128]{0,1:T(8,128)} %copy-done.12) | copy-start | bytes 1572868
  116.4 3.1 %copy-start.25 = (f32[128,64]{0,1:T(8,128)S(1)}, f32[128,64]{0,1:T(8,128)}, u32[]{:S(2)}) copy-start(f32[128,64]{0,1:T(8,128)} %param.22) | copy-start | bytes 98308
  117.5 2.0 copy-start.16
  117.5 48.9 %copy-start.5 = (f32[192,1024]{1,0:T(8,128)S(1)}, f32[192,1024]{1,0:T(8,128)}, u32[]{:S(2)}) copy-start(f32[192,1024]{1,0:T(8,128)} %copy-done.3) | copy-start | bytes 2359300
  119.5 48.9 %copy-start.11 = (f32[1,128,1024]{2,1,0:T(8,128)S(1)}, f32[1,128,1024]{2,1,0:T(8,128)}, u32[]{:S(2)}) copy-start(f32[1,128,1024]{2,1,0:T(8,128)} %param.15) | copy-start | bytes 1572868
  166.4 1.9 copy-start.17
  166.4 1.9 copy-start.20
  (3 other events, 2.5 us)
where the time goes:
time: 215 us; the launch traced here: 214 us
  blocking collectives  82.4 us (38%)
  local copies, waits for them, and re-layouts  68.9 us (32%)
  other arithmetic  24.1 us (11%)
  starting transfers between devices  17.8 us (8%)
  matrix products  16.6 us (8%)
  between operations  4.26 us (2%)
    psum x1, blocking collectives, on_device(): total_cross, total_image = lax.psum((cross_sum, image_sum), ('tm', 'space'))  42.4 us
    gather x2, local copies, waits for them, and re-layouts, operate(): jnp.take(ext_pool, column_ids, axis=1).reshape(face_dofs * 6, elements)  41.8 us
    psum x1, blocking collectives, on_device(): eta_total = lax.psum(jnp.sum(element_eta), ('tm', 'space'))  40 us
    select_n x2, other arithmetic, operate(): jnp.take(ext_pool, column_ids, axis=1).reshape(face_dofs * 6, elements)  11.7 us
    ppermute x2, starting transfers between devices, padded(): before = lax.ppermute(last, axis, up)  9.22 us
    reshape x4, local copies, waits for them, and re-layouts, operate(): trace_pool = traces.reshape(face_dofs, 6 * elements)  6.43 us
    ppermute x2, starting transfers between devices, shifted(): lax.ppermute(value, axis, [(source, source + steps) for source in range(i...  6.03 us
    select_n x2, local copies, waits for them, and re-layouts, operate(): jnp.take(ext_pool, column_ids, axis=1).reshape(face_dofs * 6, elements)  5.71 us
  transfers between devices with their start and end apart: 6, of which 0 were waited for; matrix products, arithmetic and copies ran while one was open for 38% of the time, Pallas kernels for 0%

commit v1 on v0

--- a/solution.py
+++ b/solution.py
@@ -68,7 +68,7 @@
     image, step_jump, step_time = operate(direction)
     cross_sum = jnp.sum(residual * image)
     image_sum = jnp.sum(image * image)
-    total_cross, total_image = lax.psum((cross_sum, image_sum), ("tm", "space"))
+    total_cross, total_image = lax.psum(lax.psum((cross_sum, image_sum), "space"), "tm")
     step_size = total_cross / total_image
     smoothed = start_field + step_size * direction
     new_residual = residual - step_size * image

time: 215 us -> 200 us (0.930)
  blocking collectives: 82.4 us -> 66.5 us
    psum x1 -> x2, blocking collectives: 42.4 us -> 29.5 us  [the longest x1 23.1 us: on_device(): lax.psum((cross_sum, image_sum), 'space')]
    psum x1, blocking collectives: 40 us -> 37 us  [on_device(): eta_total = lax.psum(jnp.sum(element_eta), ('tm', 'space'))]
  transfers between devices with their start and end apart: 6 -> 6, of which waited for: 0 -> 0; matrix products, arithmetic and copies ran while one was open for 38% -> 41% of each run, Pallas kernels for 0% -> 0%
where the time goes in v1:
time: 200 us; the launch traced here: 198 us
  local copies, waits for them, and re-layouts  68.9 us (34%)
  blocking collectives  66.5 us (33%)
  other arithmetic  24 us (12%)
  starting transfers between devices  17.9 us (9%)
  matrix products  16.6 us (8%)
  between operations  4.26 us (2%)
    gather x2, local copies, waits for them, and re-layouts, operate(): jnp.take(ext_pool, column_ids, axis=1).reshape(face_dofs * 6, elements)  41.9 us
    psum x1, blocking collectives, on_device(): eta_total = lax.psum(jnp.sum(element_eta), ('tm', 'space'))  37 us
    psum x1, blocking collectives, on_device(): lax.psum((cross_sum, image_sum), 'space')  23.1 us
    select_n x2, other arithmetic, operate(): jnp.take(ext_pool, column_ids, axis=1).reshape(face_dofs * 6, elements)  11.7 us
    ppermute x2, starting transfers between devices, padded(): before = lax.ppermute(last, axis, up)  9.24 us
    reshape x4, local copies, waits for them, and re-layouts, operate(): trace_pool = traces.reshape(face_dofs, 6 * elements)  6.42 us
    psum x1, blocking collectives, on_device(): lax.psum(lax.psum((cross_sum, image_sum), 'space'), 'tm')  6.37 us
    ppermute x2, starting transfers between devices, shifted(): lax.ppermute(value, axis, [(source, source + steps) for source in range(i...  6.03 us
  transfers between devices with their start and end apart: 6, of which 0 were waited for; matrix products, arithmetic and copies ran while one was open for 41% of the time, Pallas kernels for 0%

profile of v1, /device:TPU:0, one launch (start us, length us, event | category | flops | bytes accessed | tf_op | source)
XLA Modules:
  0.0 198.1 jit_solution(17310130023861153482)
XLA Ops:
  2.1 1.8 fusion.4
  6.0 2.0 copy.37
  9.6 4.9 %collective-permute-start = (f32[32,128]{0,1:T(8,128)}, f32[32,128]{0,1:T(8,128)S(1)}, u32[]{:S(2)}, u32[]{:S(2)}) collective-permute-start(f32[32,128]{0,1:T(8,128)} %get-tuple-element.13), channel_id=1, source_target_pairs={{0,1},{1,2},{2,3},{3,4},{4,5},{5,6},{6,7},{8,9},{9,10},{10,11},{11... | collective-permute-start | bytes 49160 | tf_op jit(solution)/shard_map/ppermute | solution.py:14
  14.5 1.3 collective-permute-start.1
  15.8 1.7 slice_bitcast_fusion
  17.5 2.2 %collective-permute-start.2 = (f32[64,1024]{1,0:T(8,128)}, f32[64,1024]{1,0:T(8,128)}, u32[]{:S(2)}, u32[]{:S(2)}) collective-permute-start(f32[64,1024]{1,0:T(8,128)} %slice_bitcast_fusion), channel_id=1, source_target_pairs={{0,8},{8,16},{16,24},{1,9},{9,17},{17,25},{2,10},{10,18},{18,26},{... | collective-permute-start | bytes 786440 | tf_op jit(solution)/shard_map/ppermute | solution.py:23
  20.5 2.4 %convolution_multiply_fusion.1 = f32[128,1024]{1,0:T(8,128)} fusion(f32[128,128]{1,0:T(8,128)S(1)} %copy-done.22, f32[1,128,1024]{2,1,0:T(8,128)} %param.15, f32[1024]{0:T(1024)S(1)} %copy-done.27), kind=kOutput, calls=%fused_computation.18 | convolution fusion | flops 201457664 | bytes 1118208 | tf_op jit(solution)/shard_map/dot_general | solution.py:60
  24.0 2.3 %tile.10 = f32[192,1024]{1,0:T(8,128)} reshape(f32[32,6,1024]{2,1,0:T(8,128)} %tile.4) | data formatting | bytes 1572864 | tf_op jit(solution)/shard_map/tile | solution.py:46
  26.3 2.1 %pad_maximum_fusion = f32[32,6400]{0,1:T(8,128)S(1)} fusion(f32[32,128]{0,1:T(8,128)S(1)} %collective-permute-done.1, f32[32,128]{0,1:T(8,128)S(1)} %collective-permute-done, f32[32,6144]{0,1:T(8,128)} %copy-done.1), kind=kLoop, calls=%fused_computation.4 | loop fusion | flops 409600 | bytes 1638400 | tf_op jit(solution)/shard_map/concatenate | solution.py:56
  28.4 20.9 %gather_fusion.1 = f32[6144,32]{1,0:T(8,128)} fusion(f32[32,6400]{0,1:T(8,128)S(1)} %pad_maximum_fusion, s32[6144]{0:T(1024)S(1)} %fusion.8), kind=kCustom, calls=%fused_computation.1.clone | custom fusion | bytes 1597440 | tf_op jit(solution)/shard_map/jit(_take)/gather | solution.py:57
  49.3 5.8 %select_bitcast_fusion.1 = f32[32,6144]{0,1:T(8,128)} fusion(f32[6144,32]{1,0:T(8,128)} %gather_fusion.1, pred[6144]{0:T(1024)(128)(4,1)S(1)} %compare_and_fusion), kind=kLoop, calls=%fused_computation.7 | loop fusion | flops 196608 | bytes 1579008 | tf_op jit(solution)/shard_map/jit(_take)/select_n | solution.py:57
  55.1 3.2 %copy.38 = f32[32,6144]{1,0:T(8,128)} copy(f32[32,6144]{0,1:T(8,128)} %select_bitcast_fusion.1) | data formatting | bytes 1572864 | tf_op jit(solution)/shard_map/jit(_take)/select_n | solution.py:57
  58.4 1.4 reshape.76
  59.8 1.9 fusion.2
  61.7 1.6 fusion.3
  67.3 1.3 reshape.77
  68.5 2.0 copy.40
  71.3 4.4 %collective-permute-start.3 = (f32[32,128]{0,1:T(8,128)S(1)}, f32[32,128]{0,1:T(8,128)S(1)}, u32[]{:S(2)}, u32[]{:S(2)}) collective-permute-start(f32[32,128]{0,1:T(8,128)S(1)} %get-tuple-element.11), channel_id=1, source_target_pairs={{0,1},{1,2},{2,3},{3,4},{4,5},{5,6},{6,7},{8,9},{9,10},{10,11},{11... | collective-permute-start | bytes 49160 | tf_op jit(solution)/shard_map/ppermute | solution.py:14
  75.7 1.3 collective-permute-start.4
  77.0 2.4 %convolution_multiply_fusion = f32[1024,128]{0,1:T(8,128)} fusion(f32[1024,128]{0,1:T(8,128)} %copy-done.12, f32[128,128]{1,0:T(8,128)S(1)} %copy-done.23, f32[1024]{0:T(1024)S(1)} %copy-done.27), kind=kOutput, calls=%fused_computation.14 | convolution fusion | flops 201457664 | bytes 1118208 | tf_op jit(solution)/shard_map/dot_general | solution.py:60
  79.5 1.7 slice.53
  81.2 3.9 %collective-permute-start.5 = (f32[64,1024]{1,0:T(8,128)}, f32[64,1024]{1,0:T(8,128)}, u32[]{:S(2)}, u32[]{:S(2)}) collective-permute-start(f32[64,1024]{1,0:T(8,128)} %slice.53), channel_id=1, source_target_pairs={{0,8},{8,16},{16,24},{1,9},{9,17},{17,25},{2,10},{10,18},{18,26},{... | collective-permute-start | bytes 786440 | tf_op jit(solution)/shard_map/ppermute | solution.py:23
  85.0 2.1 %pad_maximum_fusion.1 = f32[32,6400]{0,1:T(8,128)S(1)} fusion(f32[32,128]{0,1:T(8,128)S(1)} %collective-permute-done.4, f32[32,128]{0,1:T(8,128)S(1)} %collective-permute-done.3, f32[32,6144]{0,1:T(8,128)} %copy-done.2), kind=kLoop, calls=%fused_computation.5 | loop fusion | flops 409600 | bytes 1638400 | tf_op jit(solution)/shard_map/concatenate | solution.py:56
  87.2 20.9 %gather_fusion.3 = f32[6144,32]{1,0:T(8,128)} fusion(f32[32,6400]{0,1:T(8,128)S(1)} %pad_maximum_fusion.1, s32[6144]{0:T(1024)S(1)} %fusion.8), kind=kCustom, calls=%fused_computation.3.clone | custom fusion | bytes 1597440 | tf_op jit(solution)/shard_map/jit(_take)/gather | solution.py:57
  108.1 5.8 %select_bitcast_fusion = f32[32,6144]{0,1:T(8,128)} fusion(f32[6144,32]{1,0:T(8,128)} %gather_fusion.3, pred[6144]{0:T(1024)(128)(4,1)S(1)} %compare_and_fusion), kind=kLoop, calls=%fused_computation.6 | loop fusion | flops 196608 | bytes 1579008 | tf_op jit(solution)/shard_map/jit(_take)/select_n | solution.py:57
  113.9 2.5 %copy.41 = f32[32,6144]{1,0:T(8,128)S(1)} copy(f32[32,6144]{0,1:T(8,128)} %select_bitcast_fusion) | data formatting | bytes 1572864 | tf_op jit(solution)/shard_map/jit(_take)/select_n | solution.py:57
  117.5 2.0 convolution_add_fusion.1
  119.5 3.1 %multiply_reduce_fusion.2 = (f32[]{:T(128)}, f32[]{:T(128)}, f32[128,1024]{1,0:T(8,128)}) fusion(f32[128,1024]{1,0:T(8,128)S(1)} %copy-done.16, f32[1024,128]{0,1:T(8,128)S(1)} %convolution_add_fusion.1, f32[128,64]{0,1:T(8,128)S(1)} %copy-done.25, f32[64,1024]{1,0:T(8,128)} %collective-permute-done.5, f32[128,1024]{1,0:T(8,128)S(1)} %bitcast.58), kind=kOutput, calls=%fused_computation.29 | convolution fusion | flops 101384192 | bytes 2129928 | tf_op jit(solution)/shard_map/dot_general | solution.py:62
  122.6 23.1 %all-reduce = (f32[]{:T(128)}, f32[]{:T(128)}) all-reduce(f32[]{:T(128)} %get-tuple-element.6, f32[]{:T(128)} %get-tuple-element.5), channel_id=1, replica_groups=mesh['tm'=4,'space'=8] {'space'}, use_global_device_ids=true, to_apply=%region_1.4 | all-reduce | flops 2 | bytes 16 | tf_op jit(solution)/shard_map/psum | solution.py:71
  145.7 6.4 %all-reduce.1 = (f32[]{:T(128)}, f32[]{:T(128)}) all-reduce(f32[]{:T(128)} %get-tuple-element.7, f32[]{:T(128)} %get-tuple-element.8), channel_id=1, replica_groups=mesh['tm'=4,'space'=8] {'tm'}, use_global_device_ids=true, to_apply=%region_2.5 | all-reduce | flops 2 | bytes 16 | tf_op jit(solution)/shard_map/psum | solution.py:71
  153.5 1.9 multiply_reduce_fusion
  158.1 37.0 %psum.39 = f32[]{:T(128)} all-reduce(f32[]{:T(128)} %fusion.9), channel_id=1, replica_groups=mesh['tm'=4,'space'=8] {'tm','space'}, use_global_device_ids=true, to_apply=%region_10.13 | all-reduce | flops 1 | bytes 8 | tf_op jit(solution)/shard_map/psum | solution.py:82
  (87 shorter events, 16.9 us)
Async XLA Ops:
  0.6 1.4 copy-start
  4.8 14.9 %copy-start.26 = (s32[6,1024]{1,0:T(8,128)S(1)}, s32[6,1024]{1,0:T(8,128)}, u32[]{:S(2)}) copy-start(s32[6,1024]{1,0:T(8,128)} %param.23) | copy-start | bytes 73732
  4.8 15.7 %copy-start.22 = (f32[128,128]{1,0:T(8,128)S(1)}, f32[128,128]{1,0:T(8,128)}, u32[]{:S(2)}) copy-start(f32[128,128]{1,0:T(8,128)} %param.18) | copy-start | bytes 196612
  4.8 15.7 %copy-start.27 = (f32[1024]{0:T(1024)S(1)}, f32[1024]{0:T(1024)}, u32[]{:S(2)}) copy-start(f32[1024]{0:T(1024)} %param.17) | copy-start | bytes 12292
  8.0 18.3 %copy-start.1 = (f32[32,6144]{0,1:T(8,128)}, f32[32,6144]{0,1:T(8,128)S(1)}, u32[]{:S(2)}) copy-start(f32[32,6144]{0,1:T(8,128)S(1)} %copy.37) | copy-start | bytes 2359300
  9.6 16.6 %collective-permute-start = (f32[32,128]{0,1:T(8,128)}, f32[32,128]{0,1:T(8,128)S(1)}, u32[]{:S(2)}, u32[]{:S(2)}) collective-permute-start(f32[32,128]{0,1:T(8,128)} %get-tuple-element.13), channel_id=1, source_target_pairs={{0,1},{1,2},{2,3},{3,4},{4,5},{5,6},{6,7},{8,9},{9,10},{10,11},{11... | collective-permute-start | bytes 49160 | tf_op jit(solution)/shard_map/ppermute | solution.py:14
  14.5 11.8 %collective-permute-start.1 = (f32[32,128]{0,1:T(8,128)}, f32[32,128]{0,1:T(8,128)S(1)}, u32[]{:S(2)}, u32[]{:S(2)}) collective-permute-start(f32[32,128]{0,1:T(8,128)} %get-tuple-element.14), channel_id=1, source_target_pairs={{1,0},{2,1},{3,2},{4,3},{5,4},{6,5},{7,6},{9,8},{10,9},{11,10},{12... | collective-permute-start | bytes 49160 | tf_op jit(solution)/shard_map/ppermute | solution.py:15
  17.5 44.2 %collective-permute-start.2 = (f32[64,1024]{1,0:T(8,128)}, f32[64,1024]{1,0:T(8,128)}, u32[]{:S(2)}, u32[]{:S(2)}) collective-permute-start(f32[64,1024]{1,0:T(8,128)} %slice_bitcast_fusion), channel_id=1, source_target_pairs={{0,8},{8,16},{16,24},{1,9},{9,17},{17,25},{2,10},{10,18},{18,26},{... | collective-permute-start | bytes 786440 | tf_op jit(solution)/shard_map/ppermute | solution.py:23
  55.1 4.6 %copy-start.4 = (f32[192,1024]{1,0:T(8,128)S(1)}, f32[192,1024]{1,0:T(8,128)}, u32[]{:S(2)}) copy-start(f32[192,1024]{1,0:T(8,128)} %copy-done.3) | copy-start | bytes 2359300
  55.1 4.6 %copy-start.6 = (f32[192,1024]{1,0:T(8,128)S(1)}, f32[192,1024]{1,0:T(8,128)}, u32[]{:S(2)}) copy-start(f32[192,1024]{1,0:T(8,128)} %tile.10) | copy-start | bytes 2359300
  55.1 4.6 %copy-start.19 = (f32[128,1024]{1,0:T(8,128)S(1)}, f32[128,1024]{1,0:T(8,128)}, u32[]{:S(2)}) copy-start(f32[128,1024]{1,0:T(8,128)} %convolution_multiply_fusion.1) | copy-start | bytes 1572868
  58.4 3.3 %copy-start.10 = (f32[1,128,1024]{2,1,0:T(8,128)S(1)}, f32[1,128,1024]{2,1,0:T(8,128)}, u32[]{:S(2)}) copy-start(f32[1,128,1024]{2,1,0:T(8,128)} %param.15) | copy-start | bytes 1572868
  59.8 5.0 %copy-start.14 = (f32[192,1024]{1,0:T(8,128)}, f32[192,1024]{1,0:T(8,128)S(1)}, u32[]{:S(2)}) copy-start(f32[192,1024]{1,0:T(8,128)S(1)} %reshape.76) | copy-start | bytes 2359300
  59.8 1.9 copy-start.21
  59.8 1.9 copy-start.24
  59.8 4.3 %copy-start.28 = (f32[128,128]{1,0:T(8,128)S(1)}, f32[128,128]{1,0:T(8,128)}, u32[]{:S(2)}) copy-start(f32[128,128]{1,0:T(8,128)} %param.19) | copy-start | bytes 196612
  66.4 0.9 copy-start.8
  67.3 9.8 %copy-start.23 = (f32[128,128]{1,0:T(8,128)S(1)}, f32[128,128]{1,0:T(8,128)}, u32[]{:S(2)}) copy-start(f32[128,128]{1,0:T(8,128)} %param.18) | copy-start | bytes 196612
  70.5 14.6 %copy-start.2 = (f32[32,6144]{0,1:T(8,128)}, f32[32,6144]{0,1:T(8,128)S(1)}, u32[]{:S(2)}) copy-start(f32[32,6144]{0,1:T(8,128)S(1)} %copy.40) | copy-start | bytes 2359300
  71.3 13.7 %collective-permute-start.3 = (f32[32,128]{0,1:T(8,128)S(1)}, f32[32,128]{0,1:T(8,128)S(1)}, u32[]{:S(2)}, u32[]{:S(2)}) collective-permute-start(f32[32,128]{0,1:T(8,128)S(1)} %get-tuple-element.11), channel_id=1, source_target_pairs={{0,1},{1,2},{2,3},{3,4},{4,5},{5,6},{6,7},{8,9},{9,10},{10,11},{11... | collective-permute-start | bytes 49160 | tf_op jit(solution)/shard_map/ppermute | solution.py:14
  75.7 9.3 %collective-permute-start.4 = (f32[32,128]{0,1:T(8,128)S(1)}, f32[32,128]{0,1:T(8,128)S(1)}, u32[]{:S(2)}, u32[]{:S(2)}) collective-permute-start(f32[32,128]{0,1:T(8,128)S(1)} %get-tuple-element.12), channel_id=1, source_target_pairs={{1,0},{2,1},{3,2},{4,3},{5,4},{6,5},{7,6},{9,8},{10,9},{11,10},{12... | collective-permute-start | bytes 49160 | tf_op jit(solution)/shard_map/ppermute | solution.py:15
  81.2 38.3 %collective-permute-start.5 = (f32[64,1024]{1,0:T(8,128)}, f32[64,1024]{1,0:T(8,128)}, u32[]{:S(2)}, u32[]{:S(2)}) collective-permute-start(f32[64,1024]{1,0:T(8,128)} %slice.53), channel_id=1, source_target_pairs={{0,8},{8,16},{16,24},{1,9},{9,17},{17,25},{2,10},{10,18},{18,26},{... | collective-permute-start | bytes 786440 | tf_op jit(solution)/shard_map/ppermute | solution.py:23
  113.9 3.6 %copy-start.7 = (f32[192,1024]{1,0:T(8,128)S(1)}, f32[192,1024]{1,0:T(8,128)}, u32[]{:S(2)}) copy-start(f32[192,1024]{1,0:T(8,128)} %tile.10) | copy-start | bytes 2359300
  113.9 3.6 %copy-start.9 = (f32[192,1024]{1,0:T(8,128)S(1)}, f32[192,1024]{1,0:T(8,128)}, u32[]{:S(2)}) copy-start(f32[192,1024]{1,0:T(8,128)} %copy-done.8) | copy-start | bytes 2359300
  113.9 3.6 %copy-start.18 = (f32[1024,128]{0,1:T(8,128)S(1)}, f32[1024,128]{0,1:T(8,128)}, u32[]{:S(2)}) copy-start(f32[1024,128]{0,1:T(8,128)} %convolution_multiply_fusion) | copy-start | bytes 1572868
  116.4 3.1 %copy-start.13 = (f32[1024,128]{0,1:T(8,128)S(1)}, f32[1024,128]{0,1:T(8,128)}, u32[]{:S(2)}) copy-start(f32[1024,128]{0,1:T(8,128)} %copy-done.12) | copy-start | bytes 1572868
  116.4 3.1 %copy-start.25 = (f32[128,64]{0,1:T(8,128)S(1)}, f32[128,64]{0,1:T(8,128)}, u32[]{:S(2)}) copy-start(f32[128,64]{0,1:T(8,128)} %param.22) | copy-start | bytes 98308
  117.5 2.0 %copy-start.16 = (f32[128,1024]{1,0:T(8,128)S(1)}, f32[128,1024]{1,0:T(8,128)}, u32[]{:S(2)}) copy-start(f32[128,1024]{1,0:T(8,128)} %copy-done.15) | copy-start | bytes 1572868
  117.5 36.0 %copy-start.5 = (f32[192,1024]{1,0:T(8,128)S(1)}, f32[192,1024]{1,0:T(8,128)}, u32[]{:S(2)}) copy-start(f32[192,1024]{1,0:T(8,128)} %copy-done.3) | copy-start | bytes 2359300
  119.5 36.0 %copy-start.11 = (f32[1,128,1024]{2,1,0:T(8,128)S(1)}, f32[1,128,1024]{2,1,0:T(8,128)}, u32[]{:S(2)}) copy-start(f32[1,128,1024]{2,1,0:T(8,128)} %param.15) | copy-start | bytes 1572868
  153.5 1.9 copy-start.17
  153.5 1.9 copy-start.20
  (3 other events, 2.5 us)
